TPU v7x, 512 devices: a whole 4x4x16 slice. The times are simulated.
512 devices in a mesh: src: 16 (over z), tile: 8 (over x, core), gauge: 4 (over y).
Axes of the slice: x: 4, y: 4, z: 16, core: 2. Of those that a mesh axis runs over, the one named last changes fastest.
Arguments:
- responses: float32 [512, 2, 4, 128, 256], P(('src', 'tile'), None, 'gauge'), may hold values from -0.1875 to 0.1875
- footprint: int32 [512, 2], P(('src', 'tile')), may hold values from 0 to 15, all different within a row; in each aligned block of 4 rows (0 to 3, 4 to 7, ...) at most 2 rows name the same one
- theta_start: float32 [512, 8, 128], P(('src', 'tile')), may hold values from -4 to 4
- observed: float32 [128, 4, 8, 256], P(('src', 'tile'), 'gauge'), may hold values from -6 to 6
Outputs:
- theta: float32 [512, 8, 128], P(('src', 'tile'))
- misfit: float32 [128, 4, 8, 256], P(('src', 'tile'), 'gauge')
Inputs may be any that keep to these rules, and one draw needn't show every extreme that they name: `footprint`: each source's 2 entries differ. Among the 4 sources of one src and tile index, no value is named more than 2 times, a bound that some block reaches.
All inputs are finite; a program needn't handle non-finite values.
Results may differ from a plain program's by a relative error of at most 0.00017.
Values sent between devices are 32-bit elements; how exact they have to be, the bound alone decides.
A program may use at most 64 MiB of HBM per device.

v0:
```python
import jax
import jax.numpy as jnp
from jax import lax
from jax.sharding import PartitionSpec as P

GN_STEPS = 2
CG_ITERS = 2


damping = 0.1
highest = lax.Precision.HIGHEST


def local(responses, footprint, theta_start, observed):
    n_src = lax.axis_size("src")
    n_gauge = lax.axis_size("gauge")
    src_dev, foot, wins, width, length = responses.shape
    count = src_dev * foot
    blocks = responses.reshape(count, wins, width, length)
    target = footprint.reshape(count)
    dest_hot = (target[:, None] == jnp.arange(n_src, dtype=jnp.int32)[None, :]).astype(jnp.float32)
    capacity = max(2, -(-count // n_src))
    slots = n_src * capacity
    rank = jnp.sum(dest_hot * (jnp.cumsum(dest_hot, axis=0) - 1.0), axis=1).astype(jnp.int32)
    slot_of = target * capacity + rank
    slot_hot = (slot_of[:, None] == jnp.arange(slots, dtype=jnp.int32)[None, :]).astype(jnp.float32)
    observed_here = observed[0]
    packed_blocks = jnp.einsum("bq,bwkl->qwkl", slot_hot, blocks, precision=highest)
    received_blocks = lax.all_to_all(packed_blocks, "src", split_axis=0, concat_axis=0, tiled=True)

    def forward(values):
        spread = jnp.repeat(values, foot, axis=0)
        packed = jnp.einsum("bq,bek->qek", slot_hot, spread, precision=highest)
        arrived = lax.all_to_all(packed, "src", split_axis=0, concat_axis=0, tiled=True)
        return jnp.einsum("qek,qwkl->wel", arrived, received_blocks, precision=highest)

    def adjoint(field):
        backward = jnp.einsum("wel,qwkl->qek", field, received_blocks, precision=highest)
        returned = lax.all_to_all(backward, "src", split_axis=0, concat_axis=0, tiled=True)
        per_block = jnp.einsum("bq,qek->bek", slot_hot, returned, precision=highest)
        summed = jnp.sum(
            per_block.reshape(src_dev, foot, per_block.shape[1], per_block.shape[2]), axis=1
        )
        return lax.psum(summed, "gauge")

    theta = theta_start
    misfit = jnp.zeros_like(observed_here)
    for outer in range(GN_STEPS):
        coef = jax.nn.softplus(theta)
        slope = jax.nn.sigmoid(theta)
        misfit = forward(coef) - observed_here
        grad = slope * adjoint(misfit) + damping * theta
        update = jnp.zeros_like(theta)
        res = -grad
        direction = res
        norm_now = lax.psum(jnp.sum(res * res, axis=(0, 2)), ("src", "tile"))
        for inner in range(CG_ITERS):
            image = forward(slope * direction)
            norm_next = norm_now
            local_curv = (
                jnp.sum(image * image, axis=(0, 2))
                + damping * jnp.sum(direction * direction, axis=(0, 2)) / n_gauge
            )
            curv = lax.psum(local_curv, ("src", "tile", "gauge"))
            alpha = norm_now / curv
            applied = slope * adjoint(image) + damping * direction
            update = update + alpha[None, :, None] * direction
            res = res - alpha[None, :, None] * applied
            if inner + 1 < CG_ITERS:
                norm_next = lax.psum(jnp.sum(res * res, axis=(0, 2)), ("src", "tile"))
            if inner + 1 < CG_ITERS:
                direction = res + (norm_next / norm_now)[None, :, None] * direction
                norm_now = norm_next
        theta = theta + update
    return (theta, misfit[None])


def solution(mesh):
    in_specs = (
        P(("src", "tile"), None, "gauge", None, None),
        P(("src", "tile"), None),
        P(("src", "tile"), None, None),
        P(("src", "tile"), "gauge", None, None),
    )
    out_specs = (P(("src", "tile"), None, None), P(("src", "tile"), "gauge", None, None))
    return jax.shard_map(local, mesh=mesh, in_specs=in_specs, out_specs=out_specs, check_vma=False)
```

profile of v0, /device:TPU:1, one launch (start us, length us, event | category | flops | bytes accessed | tf_op | source)
XLA Modules:
  0.0 1926.5 jit_solution(504612940981126562)
XLA Ops:
  3.7 15.7 all-to-all-start.1
  31.4 6.7 all-to-all-start
  38.4 181.6 %all-to-all-done = f32[32,1,128,256]{3,2,1,0:T(8,128)} async-done(((f32[32,1,128,256]{3,2,1,0:T(8,128)}), f32[32,1,128,256]{3,2,1,0:T(8,128)}, u32[]{:S(2)}, u32[]{:S(2)}) %all-to-all-start) | async-done | bytes 4194336 | tf_op jit(solution)/shard_map/all_to_all | solution.py:29
  220.0 6.8 fusion.48
  226.8 12.1 fusion.30
  239.1 22.9 %all_to_all.55 = f32[32,8,128]{2,1,0:T(8,128)S(1)} all-to-all(f32[32,8,128]{2,1,0:T(8,128)S(1)} %copy.94), channel_id=1, replica_groups=mesh['src'=16,'tile'=8,'gauge'=4] {'src'}, dimensions={0} | all-to-all | bytes 262144 | tf_op jit(solution)/shard_map/all_to_all | solution.py:39
  262.3 13.7 psum.84
  276.6 18.1 all_to_all.56
  294.9 6.9 fusion.88
  301.8 12.1 fusion.33
  318.8 252.9 %psum.85 = f32[8]{0:T(128)S(1)} all-reduce(f32[8]{0:T(128)S(1)} %get-tuple-element.16), channel_id=1, replica_groups=mesh['src'=16,'tile'=8,'gauge'=4] {'src','tile'}, use_global_device_ids=true, to_apply=%region_5.6 | all-reduce | flops 8 | bytes 64 | tf_op jit(solution)/shard_map/psum | solution.py:56
  571.7 99.7 %psum.86 = f32[8]{0:T(128)S(1)} all-reduce(f32[8]{0:T(128)S(1)} %multiply_add_fusion.7), channel_id=1, replica_groups=mesh['src'=16,'tile'=8,'gauge'=4] {'src','tile','gauge'}, use_global_device_ids=true, to_apply=%region_7.8 | all-reduce | flops 8 | bytes 64 | tf_op jit(solution)/shard_map/psum | solution.py:64
  671.7 13.2 psum.87
  685.1 250.6 %psum.88 = f32[8]{0:T(128)S(1)} all-reduce(f32[8]{0:T(128)S(1)} %get-tuple-element.14), channel_id=1, replica_groups=mesh['src'=16,'tile'=8,'gauge'=4] {'src','tile'}, use_global_device_ids=true, to_apply=%region_11.12 | all-reduce | flops 8 | bytes 64 | tf_op jit(solution)/shard_map/psum | solution.py:70
  936.3 22.0 %all_to_all.57 = f32[32,8,128]{2,1,0:T(8,128)S(1)} all-to-all(f32[32,8,128]{2,1,0:T(8,128)S(1)} %copy.101), channel_id=1, replica_groups=mesh['src'=16,'tile'=8,'gauge'=4] {'src'}, dimensions={0} | all-to-all | bytes 262144 | tf_op jit(solution)/shard_map/all_to_all | solution.py:34
  958.6 6.5 fusion.72
  965.1 101.3 %psum.89 = f32[8]{0:T(128)S(1)} all-reduce(f32[8]{0:T(128)S(1)} %multiply_add_fusion.6), channel_id=1, replica_groups=mesh['src'=16,'tile'=8,'gauge'=4] {'src','tile','gauge'}, use_global_device_ids=true, to_apply=%region_14.15 | all-reduce | flops 8 | bytes 64 | tf_op jit(solution)/shard_map/psum | solution.py:64
  1067.0 17.0 all_to_all.58
  1084.3 6.8 fusion.60
  1091.1 12.1 fusion.36
  1103.4 17.8 all_to_all.59
  1121.4 13.2 psum.90
  1135.2 17.3 all_to_all.60
  1152.8 6.9 fusion.86
  1159.8 12.1 fusion.39
  1176.7 253.3 %psum.91 = f32[8]{0:T(128)S(1)} all-reduce(f32[8]{0:T(128)S(1)} %get-tuple-element.10), channel_id=1, replica_groups=mesh['src'=16,'tile'=8,'gauge'=4] {'src','tile'}, use_global_device_ids=true, to_apply=%region_18.19 | all-reduce | flops 8 | bytes 64 | tf_op jit(solution)/shard_map/psum | solution.py:56
  1430.1 100.1 %psum.92 = f32[8]{0:T(128)S(1)} all-reduce(f32[8]{0:T(128)S(1)} %multiply_add_fusion.5), channel_id=1, replica_groups=mesh['src'=16,'tile'=8,'gauge'=4] {'src','tile','gauge'}, use_global_device_ids=true, to_apply=%region_20.21 | all-reduce | flops 8 | bytes 64 | tf_op jit(solution)/shard_map/psum | solution.py:64
  1530.5 13.2 psum.93
  1543.9 250.6 %psum.94 = f32[8]{0:T(128)S(1)} all-reduce(f32[8]{0:T(128)S(1)} %get-tuple-element.8), channel_id=1, replica_groups=mesh['src'=16,'tile'=8,'gauge'=4] {'src','tile'}, use_global_device_ids=true, to_apply=%region_24.25 | all-reduce | flops 8 | bytes 64 | tf_op jit(solution)/shard_map/psum | solution.py:70
  1795.1 22.1 %all_to_all.61 = f32[32,8,128]{2,1,0:T(8,128)S(1)} all-to-all(f32[32,8,128]{2,1,0:T(8,128)S(1)} %copy.112), channel_id=1, replica_groups=mesh['src'=16,'tile'=8,'gauge'=4] {'src'}, dimensions={0} | all-to-all | bytes 262144 | tf_op jit(solution)/shard_map/all_to_all | solution.py:34
  1817.5 6.5 fusion.69
  1824.0 101.3 %psum.95 = f32[8]{0:T(128)S(1)} all-reduce(f32[8]{0:T(128)S(1)} %multiply_add_fusion.4), channel_id=1, replica_groups=mesh['src'=16,'tile'=8,'gauge'=4] {'src','tile','gauge'}, use_global_device_ids=true, to_apply=%region_27.28 | all-reduce | flops 8 | bytes 64 | tf_op jit(solution)/shard_map/psum | solution.py:64
  (79 shorter events, 31.9 us)
Async XLA Ops:
  0.6 18.8 copy-start
  3.7 27.7 %all-to-all-start.1 = ((f32[32,8,128]{2,1,0:T(8,128)}), f32[32,8,128]{2,1,0:T(8,128)S(1)}, u32[]{:S(2)}, u32[]{:S(2)}) async-start(f32[32,8,128]{2,1,0:T(8,128)} %copy.92), calls=%async_computation.1 | async-start | bytes 262144 | tf_op jit(solution)/shard_map/all_to_all | solution.py:34
  25.9 194.0 %copy-start.2 = (f32[1,1,8,256]{3,2,1,0:T(8,128)S(1)}, f32[1,1,8,256]{3,2,1,0:T(8,128)}, u32[]{:S(2)}) copy-start(f32[1,1,8,256]{3,2,1,0:T(8,128)} %param.7) | copy-start | bytes 24580
  31.4 188.6 %all-to-all-start = ((f32[32,1,128,256]{3,2,1,0:T(8,128)}), f32[32,1,128,256]{3,2,1,0:T(8,128)}, u32[]{:S(2)}, u32[]{:S(2)}) async-start(f32[32,1,128,256]{3,2,1,0:T(8,128)} %copy.85), calls=%async_computation | async-start | bytes 8388608 | tf_op jit(solution)/shard_map/all_to_all | solution.py:29
  38.4 237.6 %copy-start.1 = (f32[4,8,128]{2,1,0:T(8,128)S(1)}, f32[4,8,128]{2,1,0:T(8,128)}, u32[]{:S(2)}) copy-start(f32[4,8,128]{2,1,0:T(8,128)} %param.6) | copy-start | bytes 49156
  314.8 356.6 %all-to-all-start.4 = ((f32[32,8,128]{2,1,0:T(8,128)}), f32[32,8,128]{2,1,0:T(8,128)S(1)}, u32[]{:S(2)}, u32[]{:S(2)}) async-start(f32[32,8,128]{2,1,0:T(8,128)} %copy.99), calls=%async_computation.4 | async-start | bytes 262144 | tf_op jit(solution)/shard_map/all_to_all | solution.py:39
  1091.1 68.7 %copy-start.3 = (f32[1,8,256]{2,1,0:T(8,128)}, f32[1,8,256]{2,1,0:T(8,128)S(1)}, u32[]{:S(2)}) copy-start(f32[1,8,256]{2,1,0:T(8,128)S(1)} %fusion.60) | copy-start | bytes 24580
  1172.7 357.5 %all-to-all-start.9 = ((f32[32,8,128]{2,1,0:T(8,128)}), f32[32,8,128]{2,1,0:T(8,128)S(1)}, u32[]{:S(2)}, u32[]{:S(2)}) async-start(f32[32,8,128]{2,1,0:T(8,128)} %copy.110), calls=%async_computation.9 | async-start | bytes 262144 | tf_op jit(solution)/shard_map/all_to_all | solution.py:39
where the time goes:
time: 1930 us
  blocking collectives  1600 us (83%)
  waiting for transfers between devices  187 us (10%)
  matrix products  93.6 us (5%)
  starting transfers between devices  30.5 us (2%)
    psum x2, blocking collectives, local(): norm_now = lax.psum(jnp.sum(res * res, axis=(0, 2)), ('src', 'tile'))  506 us
    psum x2, blocking collectives, local(): norm_next = lax.psum(jnp.sum(res * res, axis=(0, 2)), ('src', 'tile'))  501 us
    psum x4, blocking collectives, local(): curv = lax.psum(local_curv, ('src', 'tile', 'gauge'))  402 us
    all_to_all x1, waiting for transfers between devices, local(): lax.all_to_all(packed_blocks, 'src', split_axis=0, concat_axis=0, tiled=T...  182 us
    all_to_all x5, blocking collectives, forward(): lax.all_to_all(packed, 'src', split_axis=0, concat_axis=0, tiled=True)  96.6 us
    psum x4, blocking collectives, adjoint(): return lax.psum(summed, 'gauge')  53.3 us
    dot_general x4, matrix products, adjoint(): jnp.einsum('wel,qwkl->qek', field, received_blocks, precision=highest)  48.3 us
    all_to_all x2, blocking collectives, adjoint(): lax.all_to_all(backward, 'src', split_axis=0, concat_axis=0, tiled=True)  40.7 us
  transfers between devices with their start and end apart: 4, of which 2 were waited for; matrix products, arithmetic and copies ran while one was open for 0% of the time, Pallas kernels for 0%

commit v1 on v0

v1 whole, which is shorter than its diff:
```python
import functools

import jax
import jax.numpy as jnp
from jax import lax
from jax.experimental import pallas as pl
from jax.experimental.pallas import tpu as pltpu
from jax.sharding import PartitionSpec as P

GN_STEPS = 2
DAMPING = 0.1
MESH = pl.DeviceIdType.MESH
F32 = jnp.float32
BF16 = jnp.bfloat16


def split(x):
    hi = x.astype(BF16)
    return hi, (x - hi.astype(F32)).astype(BF16)


def far_first(n):
    return sorted(range(1, n), key=lambda j: (-min(j, n - j), j))


def kernel(
    sizes,
    resp_ref, foot_ref, theta0_ref, obs_ref,
    theta_ref, misfit_ref,
    raw, w,
    terms, arrived, rows_out, rows_in,
    field, gathered_m, gathered_b,
    scal_out, scal_in,
    tile1, tile2,
    adj_g, adj_p, curv_y, last_y,
    load_sem, z_send, z_recv, row_send, row_recv, f_send, f_recv,
    s_send, s_recv, t_send, t_recv, y_send, y_recv, c_send, c_recv,
):
    n_src, n_tile, n_gauge, src_dev, foot = sizes
    blocks = src_dev * foot
    ens, width = theta0_ref.shape[1:]
    length = obs_ref.shape[1]
    me = {"src": lax.axis_index("src"), "tile": lax.axis_index("tile"), "gauge": lax.axis_index("gauge")}
    count = {"src": n_src, "tile": n_tile, "gauge": n_gauge}

    def peers(axis):
        n = count[axis]
        return [lax.rem(me[axis] + j, n) for j in far_first(n)]

    barrier = pltpu.get_barrier_semaphore()
    for axis in ("src", "tile", "gauge"):
        for peer in peers(axis):
            pl.semaphore_signal(barrier, inc=1, device_id={axis: peer}, device_id_type=MESH)

    load = pltpu.make_async_copy(resp_ref, raw, load_sem)
    load.start()
    load.wait()
    for b in range(blocks):
        hi, lo = split(raw[b])
        w[b, 0:width, :] = hi
        w[b, width:2 * width, :] = lo

    pl.semaphore_wait(barrier, n_src + n_tile + n_gauge - 3)

    lanes = lax.broadcasted_iota(jnp.int32, (ens, 128), 1)
    sub = lax.broadcasted_iota(jnp.int32, (ens, 128), 0)

    def to_row(values):
        out = jnp.zeros((ens, 128), F32)
        for i, v in enumerate(values):
            out = out + jnp.where(lanes == sub + i * ens, v, 0.0)
        return jnp.sum(out, axis=0, keepdims=True)

    def from_row(row, i):
        return jnp.sum(jnp.where(lanes == sub + i * ens, row, 0.0), axis=1, keepdims=True)

    def send(axis, src_of, dst, send_sem, recv_sem):
        for peer in peers(axis):
            pltpu.make_async_remote_copy(
                src_ref=src_of(peer), dst_ref=dst.at[me[axis]], send_sem=send_sem, recv_sem=recv_sem,
                device_id={axis: peer}, device_id_type=MESH,
            ).start()

    def drain(ref, sem, n):
        part = ref.at[pl.ds(0, n - 1)]
        pltpu.make_async_copy(part, part, sem).wait()

    def sum_of(ref, n):
        total = ref[0]
        for i in range(1, n):
            total = total + ref[i]
        return total

    def dot_square(a, b):
        return jnp.sum(a * b, axis=tuple(range(a.ndim - 2)) + (a.ndim - 1,)).reshape(ens, 1)

    def forward_terms(x):
        outs = []
        for s in range(src_dev):
            hi, lo = split(x[s])
            left = jnp.concatenate(
                [jnp.concatenate([hi, hi], axis=1), jnp.concatenate([lo, lo], axis=1)], axis=0
            )
            for f in range(foot):
                out = jnp.dot(left, w[s * foot + f], preferred_element_type=F32)
                outs.append(out[0:ens] + out[ens:2 * ens])
        for t in range(n_src):
            total = jnp.zeros((ens, length), F32)
            for b in range(blocks):
                total = total + jnp.where(jnp.full((ens, length), foot_ref[b], jnp.int32) == t, outs[b], 0.0)
            terms[t] = total

    def forward(x, row):
        forward_terms(x)
        send("src", lambda peer: terms.at[peer], arrived, z_send, z_recv)
        if row is not None:
            rows_out[0] = row
            send("src", lambda peer: rows_out.at[0], rows_in, row_send, row_recv)
            rows_in[me["src"]] = row
        arrived[me["src"]] = terms[me["src"]]
        drain(arrived, z_recv, n_src)
        image = sum_of(arrived, n_src)
        row_sum = None
        if row is not None:
            drain(rows_in, row_recv, n_src)
            row_sum = sum_of(rows_in, n_src)
            drain(rows_in, row_send, n_src)
        drain(terms, z_send, n_src)
        return image, row_sum

    def gather(value, dst):
        field[0] = value
        send("src", lambda peer: field.at[0], dst, f_send, f_recv)
        dst[me["src"]] = value
        drain(dst, f_recv, n_src)
        drain(dst, f_send, n_src)

    def adjoint_terms(src, dst):
        mine = me["gauge"]
        for s in range(src_dev):
            total = None
            for f in range(foot):
                b = s * foot + f
                hi, lo = split(src[foot_ref[b]])
                out = lax.dot_general(
                    jnp.concatenate([hi, lo], axis=0), w[b], (((1,), (1,)), ((), ())), preferred_element_type=F32
                )
                out = out[0:ens] + out[ens:2 * ens]
                out = out[:, 0:width] + out[:, width:2 * width]
                total = out if total is None else total + out
            dst[mine, s] = total

    def gauge_sum(dst, i):
        send("gauge", lambda peer: dst.at[me["gauge"]], dst, y_send.at[i], y_recv.at[i])

        def finish():
            drain(dst, y_recv.at[i], n_gauge)
            total = sum_of(dst, n_gauge)
            drain(dst, y_send.at[i], n_gauge)
            return total

        return finish

    def row_exchange(axis, row, out, dst, send_sem, recv_sem):
        out[0] = row
        send(axis, lambda peer: out.at[0], dst, send_sem, recv_sem)
        dst[me[axis]] = row

        def finish():
            drain(dst, recv_sem, count[axis])
            total = sum_of(dst, count[axis])
            drain(dst, send_sem, count[axis])
            return total

        return finish

    theta_ref[...] = theta0_ref[...]

    def step(outer, carry):
        theta = theta_ref[...]
        slope = jax.nn.sigmoid(theta)
        coef = jnp.maximum(theta, 0.0) + jnp.log1p(jnp.exp(-jnp.abs(theta)))

        predicted, _ = forward(coef, None)
        misfit = predicted - obs_ref[...]
        misfit_ref[...] = misfit
        gather(misfit, gathered_m)
        adjoint_terms(gathered_m, adj_g)
        d0 = -(slope * gauge_sum(adj_g, 0)() + DAMPING * theta)

        b0, rr_row = forward(slope * d0, to_row([dot_square(d0, d0)]))
        gather(b0, gathered_b)
        squares = jnp.zeros((ens, length), F32)
        for t in range(n_src):
            squares = squares + gathered_b[t] * gathered_b[t]
        bb = jnp.sum(squares, axis=1, keepdims=True)
        finish_tile = row_exchange(
            "tile", to_row([bb]) + jnp.where(lanes[0:1] < ens, 0.0, pltpu.roll(rr_row, ens, 1)),
            scal_out.at[pl.ds(0, 1)], tile1, t_send.at[0], t_recv.at[0],
        )
        adjoint_terms(gathered_b, adj_p)
        finish_y = gauge_sum(adj_p, 1)
        tile_row = finish_tile()
        finish_c = row_exchange("gauge", tile_row, scal_out.at[pl.ds(1, 1)], curv_y, c_send.at[0], c_recv.at[0])
        p = slope * finish_y() + DAMPING * d0
        bb = from_row(finish_c(), 0)
        rr0 = from_row(tile_row, 1)
        alpha0 = rr0 / (bb + DAMPING * rr0)
        res = d0 - alpha0[None] * p

        image, own_row = forward(slope * res, to_row([dot_square(res, res), dot_square(res, d0)]))
        finish_z = row_exchange(
            "src", to_row([dot_square(image, image), dot_square(image, b0)]),
            scal_out.at[pl.ds(2, 1)], scal_in, s_send, s_recv,
        )
        z_row = finish_z()
        finish_tile = row_exchange(
            "tile", z_row + jnp.where(lanes[0:1] < 2 * ens, 0.0, pltpu.roll(own_row, 2 * ens, 1)),
            scal_out.at[pl.ds(3, 1)], tile2, t_send.at[1], t_recv.at[1],
        )
        tile_row = finish_tile()
        finish_c = row_exchange("gauge", tile_row, scal_out.at[pl.ds(4, 1)], last_y, c_send.at[1], c_recv.at[1])
        all_row = finish_c()
        cc, cb = from_row(all_row, 0), from_row(all_row, 1)
        rr1, rd = from_row(tile_row, 2), from_row(tile_row, 3)
        beta = rr1 / rr0
        curv = cc + beta * (2.0 * cb + beta * bb) + DAMPING * (rr1 + beta * (2.0 * rd + beta * rr0))
        alpha1 = rr1 / curv
        update = alpha0[None] * d0 + alpha1[None] * (res + beta[None] * d0)
        theta_ref[...] = theta + update
        return carry

    lax.fori_loop(0, GN_STEPS, step, 0)


def local(sizes, responses, footprint, theta_start, observed):
    n_src, n_tile, n_gauge = sizes
    src_dev, foot, _, width, length = responses.shape
    ens = theta_start.shape[1]
    blocks = src_dev * foot
    vmem = pl.BlockSpec(memory_space=pltpu.VMEM)
    dma = pltpu.SemaphoreType.DMA
    row = (1, 128)
    theta, misfit = pl.pallas_call(
        functools.partial(kernel, (n_src, n_tile, n_gauge, src_dev, foot)),
        out_shape=(
            jax.ShapeDtypeStruct(theta_start.shape, F32),
            jax.ShapeDtypeStruct((ens, length), F32),
        ),
        in_specs=[pl.BlockSpec(memory_space=pl.ANY), pl.BlockSpec(memory_space=pltpu.SMEM), vmem, vmem],
        out_specs=(vmem, vmem),
        scratch_shapes=[
            pltpu.VMEM((blocks, width, length), F32),
            pltpu.VMEM((blocks, 2 * width, length), BF16),
            pltpu.VMEM((n_src, ens, length), F32),
            pltpu.VMEM((n_src, ens, length), F32),
            pltpu.VMEM((1,) + row, F32),
            pltpu.VMEM((n_src,) + row, F32),
            pltpu.VMEM((1, ens, length), F32),
            pltpu.VMEM((n_src, ens, length), F32),
            pltpu.VMEM((n_src, ens, length), F32),
            pltpu.VMEM((5,) + row, F32),
            pltpu.VMEM((n_src,) + row, F32),
            pltpu.VMEM((n_tile,) + row, F32),
            pltpu.VMEM((n_tile,) + row, F32),
            pltpu.VMEM((n_gauge, src_dev, ens, width), F32),
            pltpu.VMEM((n_gauge, src_dev, ens, width), F32),
            pltpu.VMEM((n_gauge,) + row, F32),
            pltpu.VMEM((n_gauge,) + row, F32),
            dma, dma, dma, dma, dma, dma, dma,
            dma, dma, dma((2,)), dma((2,)), dma((2,)), dma((2,)), dma((2,)), dma((2,)),
        ],
        compiler_params=pltpu.CompilerParams(collective_id=0, has_side_effects=True),
    )(
        responses.reshape(blocks, width, length),
        footprint.reshape(blocks),
        theta_start,
        observed.reshape(ens, length),
    )
    return theta, misfit.reshape(observed.shape)


def solution(mesh):
    sizes = (mesh.shape["src"], mesh.shape["tile"], mesh.shape["gauge"])
    in_specs = (
        P(("src", "tile"), None, "gauge", None, None),
        P(("src", "tile"), None),
        P(("src", "tile"), None, None),
        P(("src", "tile"), "gauge", None, None),
    )
    out_specs = (P(("src", "tile"), None, None), P(("src", "tile"), "gauge", None, None))
    return jax.shard_map(
        functools.partial(local, sizes), mesh=mesh, in_specs=in_specs, out_specs=out_specs, check_vma=False
    )
```

time: 1930 us -> 161 us (0.08)
  blocking collectives: 1600 us -> 0 us
  waiting for transfers between devices: 187 us -> 0 us
  Pallas kernels: 0 us -> 156 us
  matrix products: 93.6 us -> 0 us
  starting transfers between devices: 30.5 us -> 0 us
    psum x12 -> x0, blocking collectives: 1460 us -> none  [the longest x2 506 us: local(): norm_now = lax.psum(jnp.sum(res * res, axis=(0, 2)), ('src', 'tile'))]
    all_to_all x4 -> x0, waiting for transfers between devices: 187 us -> none  [the longest x1 182 us: local(): lax.all_to_all(packed_blocks, 'src', split_axis=0, concat_axis=0, tiled=T...]
    pallas_call x0 -> x1, Pallas kernels: none -> 156 us  [local(): pl.pallas_call(functools.partial(kernel, (n_src, n_tile, n_gauge, src_dev...]
    all_to_all x7 -> x0, blocking collectives: 137 us -> none  [the longest x5 96.6 us: forward(): lax.all_to_all(packed, 'src', split_axis=0, concat_axis=0, tiled=True)]
    dot_general x21 -> x0, matrix products: 93.6 us -> none  [the longest x4 48.3 us: adjoint(): jnp.einsum('wel,qwkl->qek', field, received_blocks, precision=highest)]
    all_to_all x4 -> x0, starting transfers between devices: 30.5 us -> none  [the longest x1 15.7 us: forward(): lax.all_to_all(packed, 'src', split_axis=0, concat_axis=0, tiled=True)]
  transfers between devices with their start and end apart: 4 -> 0, of which waited for: 2 -> 0; matrix products, arithmetic and copies ran while one was open for 0% -> 0% of each run, Pallas kernels for 0% -> 0%
where the time goes in v1:
time: 161 us; the launch traced here: 160 us
  Pallas kernels  156 us (97%)
  local copies, waits for them, and re-layouts  3.29 us (2%)
    pallas_call x1, Pallas kernels, local(): pl.pallas_call(functools.partial(kernel, (n_src, n_tile, n_gauge, src_dev...  156 us

profile of v1, /device:TPU:1, one launch (start us, length us, event | category | flops | bytes accessed | tf_op | source)
XLA Modules:
  0.0 160.3 jit_solution(18308321254541764050)
XLA Ops:
  0.6 0.0 copy-start.1
  0.6 0.7 copy-done.1
  1.3 0.1 copy.7
  1.4 0.6 reshape.17.foot_ref
  2.0 156.3 %shard_map.59 = (f32[4,8,128]{2,1,0:T(8,128)}, f32[8,256]{1,0:T(8,128)}) custom-call(f32[8,128,256]{2,1,0:T(8,128)} %bitcast.3, s32[8]{0:T(128)} %reshape.17.foot_ref, f32[4,8,128]{2,1,0:T(8,128)} %theta0_ref.1, f32[8,256]{1,0:T(8,128)} %bitcast.4), custom_call_target="tpu_custom_call" | custom-call | tf_op jit(solution)/shard_map/pallas_call | solution.py:244
  158.3 0.0 copy-start
  158.4 1.3 copy.10
  159.7 0.0 copy-done
  159.7 0.6 copy.11
Async XLA Ops:
  0.6 0.7 copy-start.1
  158.3 1.3 copy-start

commit v2 on v1

v2 whole, which is shorter than its diff:
```python
import functools

import jax
import jax.numpy as jnp
from jax import lax
from jax.experimental import pallas as pl
from jax.experimental.pallas import tpu as pltpu
from jax.sharding import PartitionSpec as P

GN_STEPS = 2
DAMPING = 0.1
MESH = pl.DeviceIdType.MESH
F32 = jnp.float32
BF16 = jnp.bfloat16


def split(x):
    hi = x.astype(BF16)
    return hi, (x - hi.astype(F32)).astype(BF16)


def far_first(n):
    return sorted(range(1, n), key=lambda j: (-min(j, n - j), j))


def kernel(
    sizes,
    resp_hbm, foot_hbm, theta_hbm, obs_hbm,
    theta_ref, misfit_ref,
    raw, w, foot_ref, theta0, obs,
    terms, arrived, rows_out, rows_in,
    field, gathered_m, gathered_b,
    adj_g, adj_p, scal_in, plane_a, plane_b,
    load_sem, z_send, z_recv, f_send, f_recv, y_send, y_recv, r_send, r_recv, p_send, p_recv,
):
    n_src, n_tile, n_gauge, src_dev, foot = sizes
    blocks = src_dev * foot
    ens, width = theta0.shape[1:]
    length = obs.shape[1]
    my_src, my_tile, my_gauge = lax.axis_index("src"), lax.axis_index("tile"), lax.axis_index("gauge")

    src_peers = [lax.rem(my_src + j, n_src) for j in far_first(n_src)]
    gauge_peers = [lax.rem(my_gauge + j, n_gauge) for j in far_first(n_gauge)]

    def hops(ab):
        a, b = ab[0] // 2, ab[1]
        return -(min(a, n_tile // 2 - a) + min(b, n_gauge - b))

    plane_peers = [
        {"tile": lax.rem(my_tile + a, n_tile), "gauge": lax.rem(my_gauge + b, n_gauge)}
        for a, b in sorted([(a, b) for a in range(n_tile) for b in range(n_gauge) if a or b], key=hops)
    ]
    my_plane = my_tile * n_gauge + my_gauge
    n_plane = n_tile * n_gauge

    barrier = pltpu.get_barrier_semaphore()
    for peer in [{"src": p} for p in src_peers] + plane_peers:
        pl.semaphore_signal(barrier, inc=1, device_id=peer, device_id_type=MESH)

    loads = [
        pltpu.make_async_copy(a, b, load_sem.at[i])
        for i, (a, b) in enumerate(
            [(theta_hbm, theta0), (resp_hbm, raw), (foot_hbm, foot_ref), (obs_hbm, obs)]
        )
    ]
    for load in loads:
        load.start()

    lanes = lax.broadcasted_iota(jnp.int32, (ens, 128), 1)
    sub = lax.broadcasted_iota(jnp.int32, (ens, 128), 0)

    def to_row(values):
        out = jnp.zeros((ens, 128), F32)
        for i, v in enumerate(values):
            out = out + jnp.where(lanes == sub + i * ens, v, 0.0)
        return jnp.sum(out, axis=0, keepdims=True)

    def from_row(row, i):
        return jnp.sum(jnp.where(lanes == sub + i * ens, row, 0.0), axis=1, keepdims=True)

    def copy(src, dst, send_sem, recv_sem, peer):
        pltpu.make_async_remote_copy(
            src_ref=src, dst_ref=dst, send_sem=send_sem, recv_sem=recv_sem,
            device_id=peer, device_id_type=MESH,
        ).start()

    def drain(ref, sem, n):
        part = ref.at[pl.ds(0, n - 1)]
        pltpu.make_async_copy(part, part, sem).wait()

    def sum_of(ref, n):
        parts = [ref[i] for i in range(n)]
        while len(parts) > 1:
            parts = [sum(parts[i:i + 2]) for i in range(0, len(parts), 2)]
        return parts[0]

    def inner(a, b):
        prod = a * b
        if prod.ndim == 3:
            prod = sum(prod[i] for i in range(prod.shape[0]))
        return jnp.sum(prod, axis=1, keepdims=True)

    def forward_terms(x):
        outs = []
        for s in range(src_dev):
            hi, lo = split(x[s])
            left = jnp.concatenate(
                [jnp.concatenate([hi, hi], axis=1), jnp.concatenate([lo, lo], axis=1)], axis=0
            )
            for f in range(foot):
                out = jnp.dot(left, w[s * foot + f], preferred_element_type=F32)
                outs.append(out[0:ens] + out[ens:2 * ens])
        for t in range(n_src):
            total = jnp.zeros((ens, length), F32)
            for b in range(blocks):
                mine = jnp.full((ens, length), foot_ref[b % foot, b // foot], jnp.int32) == t
                total = total + jnp.where(mine, outs[b], 0.0)
            terms[t] = total

    def scatter_start():
        for peer in src_peers:
            copy(terms.at[peer], arrived.at[my_src], z_send, z_recv, {"src": peer})
        arrived[my_src] = terms[my_src]

    def scatter_finish():
        drain(arrived, z_recv, n_src)
        return sum_of(arrived, n_src)

    def gather_start(value, dst):
        field[0] = value
        for peer in src_peers:
            copy(field.at[0], dst.at[my_src], f_send, f_recv, {"src": peer})
        dst[my_src] = value

    def adjoint_terms(src, dst):
        for s in range(src_dev):
            total = None
            for f in range(foot):
                hi, lo = split(src[foot_ref[f, s]])
                out = lax.dot_general(
                    jnp.concatenate([hi, lo], axis=0), w[s * foot + f],
                    (((1,), (1,)), ((), ())), preferred_element_type=F32,
                )
                out = out[0:ens] + out[ens:2 * ens]
                out = out[:, 0:width] + out[:, width:2 * width]
                total = out if total is None else total + out
            dst[my_gauge, s] = total

    def gauge_start(dst, i):
        for peer in gauge_peers:
            copy(dst.at[my_gauge], dst.at[my_gauge], y_send.at[i], y_recv.at[i], {"gauge": peer})

    def gauge_finish(dst, i):
        drain(dst, y_recv.at[i], n_gauge)
        return sum_of(dst, n_gauge)

    def rows_start(row, dst, i):
        rows_out[i] = row
        for peer in src_peers:
            copy(rows_out.at[i], dst.at[my_src], r_send.at[i], r_recv.at[i], {"src": peer})
        dst[my_src] = row

    def rows_finish(dst, i):
        drain(dst, r_recv.at[i], n_src)
        return sum_of(dst, n_src)

    def plane_start(row, dst, i):
        rows_out[2 + i] = row
        for peer in plane_peers:
            copy(rows_out.at[2 + i], dst.at[my_plane], p_send.at[i], p_recv.at[i], peer)
        dst[my_plane] = row

    def plane_finish(dst, i):
        drain(dst, p_recv.at[i], n_plane)
        return sum_of(dst, n_plane)

    for i in (0, 1, 2):
        loads[i].wait()
    for b in range(blocks):
        hi, lo = split(raw[b])
        w[b, 0:width, :] = hi
        w[b, width:2 * width, :] = lo
    theta = theta0[...]

    for outer in range(GN_STEPS):
        slope = jax.nn.sigmoid(theta)
        coef = jnp.maximum(theta, 0.0) + jnp.log1p(jnp.exp(-jnp.abs(theta)))

        forward_terms(coef)
        if outer == 0:
            pl.semaphore_wait(barrier, n_src + n_plane - 2)
        scatter_start()
        if outer == 0:
            loads[3].wait()
        misfit = scatter_finish() - obs[...]
        gather_start(misfit, gathered_m)
        if outer + 1 == GN_STEPS:
            misfit_ref[...] = misfit
        drain(terms, z_send, n_src)
        drain(gathered_m, f_recv, n_src)
        adjoint_terms(gathered_m, adj_g)
        gauge_start(adj_g, 0)
        drain(gathered_m, f_send, n_src)
        d0 = -(slope * gauge_finish(adj_g, 0) + DAMPING * theta)

        forward_terms(slope * d0)
        scatter_start()
        rows_start(to_row([inner(d0, d0)]), rows_in, 0)
        drain(adj_g, y_send.at[0], n_gauge)
        b0 = scatter_finish()
        gather_start(b0, gathered_b)
        drain(terms, z_send, n_src)
        rr_row = rows_finish(rows_in, 0)
        drain(rows_in, r_send.at[0], n_src)
        drain(gathered_b, f_recv, n_src)
        adjoint_terms(gathered_b, adj_p)
        gauge_start(adj_p, 1)
        squares = gathered_b[0] * gathered_b[0]
        for t in range(1, n_src):
            squares = squares + gathered_b[t] * gathered_b[t]
        bb_row = to_row([jnp.sum(squares, axis=1, keepdims=True)])
        plane_start(bb_row + jnp.where(lanes[0:1] < ens, 0.0, pltpu.roll(rr_row, ens, 1)), plane_a, 0)
        drain(gathered_b, f_send, n_src)
        p = slope * gauge_finish(adj_p, 1) + DAMPING * d0

        forward_terms(slope * p)
        scatter_start()
        drain(adj_p, y_send.at[1], n_gauge)
        row = plane_finish(plane_a, 0)
        bb, rr0 = from_row(row, 0), from_row(row, 1) * (1.0 / n_gauge)
        alpha0 = rr0 / (bb + DAMPING * rr0)
        res = d0 - alpha0[None] * p
        rr1, rd = inner(res, res), inner(res, d0)
        drain(plane_a, p_send.at[0], n_plane)
        image = b0 - alpha0 * scatter_finish()
        rows_start(to_row([inner(image, image), inner(image, b0), rr1, rd]), scal_in, 1)
        drain(terms, z_send, n_src)
        plane_start(rows_finish(scal_in, 1), plane_b, 1)
        drain(scal_in, r_send.at[1], n_src)
        row = plane_finish(plane_b, 1)
        cc, cb = from_row(row, 0), from_row(row, 1)
        rr1, rd = from_row(row, 2) * (1.0 / n_gauge), from_row(row, 3) * (1.0 / n_gauge)
        beta = rr1 / rr0
        curv = cc + beta * (2.0 * cb + beta * bb) + DAMPING * (rr1 + beta * (2.0 * rd + beta * rr0))
        alpha1 = rr1 / curv
        theta = theta + (alpha0[None] * d0 + alpha1[None] * (res + beta[None] * d0))
        drain(plane_b, p_send.at[1], n_plane)
    theta_ref[...] = theta


def local(sizes, responses, footprint, theta_start, observed):
    n_src, n_tile, n_gauge = sizes
    src_dev, foot, _, width, length = responses.shape
    ens = theta_start.shape[1]
    blocks = src_dev * foot
    vmem, anywhere = pl.BlockSpec(memory_space=pltpu.VMEM), pl.BlockSpec(memory_space=pl.ANY)
    dma = pltpu.SemaphoreType.DMA
    row = (1, 128)
    theta, misfit = pl.pallas_call(
        functools.partial(kernel, (n_src, n_tile, n_gauge, src_dev, foot)),
        out_shape=(
            jax.ShapeDtypeStruct(theta_start.shape, F32),
            jax.ShapeDtypeStruct((ens, length), F32),
        ),
        in_specs=[anywhere] * 4,
        out_specs=(vmem, vmem),
        scratch_shapes=[
            pltpu.VMEM((blocks, width, length), F32),
            pltpu.VMEM((blocks, 2 * width, length), BF16),
            pltpu.SMEM((foot, src_dev), jnp.int32),
            pltpu.VMEM((src_dev, ens, width), F32),
            pltpu.VMEM((ens, length), F32),
            pltpu.VMEM((n_src, ens, length), F32),
            pltpu.VMEM((n_src, ens, length), F32),
            pltpu.VMEM((4,) + row, F32),
            pltpu.VMEM((n_src,) + row, F32),
            pltpu.VMEM((1, ens, length), F32),
            pltpu.VMEM((n_src, ens, length), F32),
            pltpu.VMEM((n_src, ens, length), F32),
            pltpu.VMEM((n_gauge, src_dev, ens, width), F32),
            pltpu.VMEM((n_gauge, src_dev, ens, width), F32),
            pltpu.VMEM((n_src,) + row, F32),
            pltpu.VMEM((n_tile * n_gauge,) + row, F32),
            pltpu.VMEM((n_tile * n_gauge,) + row, F32),
            dma((4,)), dma, dma, dma, dma,
            dma((2,)), dma((2,)), dma((2,)), dma((2,)), dma((2,)), dma((2,)),
        ],
        compiler_params=pltpu.CompilerParams(collective_id=0, has_side_effects=True),
    )(
        responses.reshape(blocks, width, length),
        footprint.T,
        theta_start,
        observed.reshape(ens, length),
    )
    return theta, misfit.reshape(observed.shape)


def solution(mesh):
    sizes = (mesh.shape["src"], mesh.shape["tile"], mesh.shape["gauge"])
    in_specs = (
        P(("src", "tile"), None, "gauge", None, None),
        P(("src", "tile"), None),
        P(("src", "tile"), None, None),
        P(("src", "tile"), "gauge", None, None),
    )
    out_specs = (P(("src", "tile"), None, None), P(("src", "tile"), "gauge", None, None))
    return jax.shard_map(
        functools.partial(local, sizes), mesh=mesh, in_specs=in_specs, out_specs=out_specs, check_vma=False
    )
```

time: 161 us -> 139 us (0.86)
  Pallas kernels: 156 us -> 137 us
    pallas_call x1, Pallas kernels: 156 us -> 137 us  [local(): pl.pallas_call(functools.partial(kernel, (n_src, n_tile, n_gauge, src_dev...]
where the time goes in v2:
time: 139 us
  Pallas kernels  137 us (99%)
  local copies, waits for them, and re-layouts  1.93 us (1%)
    pallas_call x1, Pallas kernels, local(): pl.pallas_call(functools.partial(kernel, (n_src, n_tile, n_gauge, src_dev...  137 us

profile of v2, /device:TPU:1, one launch (start us, length us, event | category | flops | bytes accessed | tf_op | source)
XLA Modules:
  0.0 139.2 jit_solution(796169259675685238)
XLA Ops:
  0.6 136.6 %shard_map.59 = (f32[4,8,128]{2,1,0:T(8,128)}, f32[8,256]{1,0:T(8,128)}) custom-call(f32[8,128,256]{2,1,0:T(8,128)} %bitcast.4, s32[2,4]{1,0:T(2,128)} %bitcast.7, f32[4,8,128]{2,1,0:T(8,128)} %theta_hbm.1, f32[8,256]{1,0:T(8,128)} %bitcast.5), custom_call_target="tpu_custom_call" | custom-call | tf_op jit(solution)/shard_map/pallas_call | solution.py:259
  137.2 0.0 copy-start
  137.2 1.3 copy.8
  138.6 0.0 copy-done
  138.6 0.6 copy.9
Async XLA Ops:
  137.2 1.3 copy-start

commit v3 on v2

--- a/solution.py
+++ b/solution.py
@@ -30,8 +30,8 @@
     raw, w, foot_ref, theta0, obs,
     terms, arrived, rows_out, rows_in,
     field, gathered_m, gathered_b,
-    adj_g, adj_p, scal_in, plane_a, plane_b,
-    load_sem, z_send, z_recv, f_send, f_recv, y_send, y_recv, r_send, r_recv, p_send, p_recv,
+    adj_g, adj_p, scal_in, plane_a, plane_b, relayed, joined,
+    load_sem, relay_send, relay_recv, z_send, z_recv, f_send, f_recv, y_send, y_recv, r_send, r_recv, p_send, p_recv,
 ):
     n_src, n_tile, n_gauge, src_dev, foot = sizes
     blocks = src_dev * foot
@@ -39,7 +39,14 @@
     length = obs.shape[1]
     my_src, my_tile, my_gauge = lax.axis_index("src"), lax.axis_index("tile"), lax.axis_index("gauge")
 
-    src_peers = [lax.rem(my_src + j, n_src) for j in far_first(n_src)]
+    turn = 1 - 2 * lax.rem(my_tile, 2)
+
+    def at(j):
+        return lax.rem(my_src + n_src + turn * j, n_src)
+
+    near = n_src // 4
+    near_js = [sign * j for j in range(near, 0, -1) for sign in (1, -1)]
+    src_peers = [at(j) for j in far_first(n_src)]
     gauge_peers = [lax.rem(my_gauge + j, n_gauge) for j in far_first(n_gauge)]
 
     def hops(ab):
@@ -54,7 +61,7 @@
     n_plane = n_tile * n_gauge
 
     barrier = pltpu.get_barrier_semaphore()
-    for peer in [{"src": p} for p in src_peers] + plane_peers:
+    for peer in [{"src": at(j)} for j in near_js] + plane_peers:
         pl.semaphore_signal(barrier, inc=1, device_id=peer, device_id_type=MESH)
 
     loads = [
@@ -117,6 +124,29 @@
                 total = total + jnp.where(mine, outs[b], 0.0)
             terms[t] = total
 
+    def first_scatter():
+        for j in range(2 * near, near, -1):
+            copy(terms.at[at(j)], relayed.at[j - near - 1], relay_send, relay_recv.at[0], {"src": at(near)})
+            if j < 2 * near:
+                copy(terms.at[at(-j)], relayed.at[j - 1], relay_send, relay_recv.at[1], {"src": at(-near)})
+        copy(terms.at[at(-near)], arrived.at[my_src], z_send, z_recv, {"src": at(-near)})
+        for side, sign, first, n in ((0, 1, 0, near), (1, -1, near, near - 1)):
+            if n == 0:
+                continue
+            part = relayed.at[pl.ds(first, n)]
+            pltpu.make_async_copy(part, part, relay_recv.at[side]).wait()
+            for j in range(n, 0, -1):
+                slot = first + j - 1
+                joined[slot] = relayed[slot] + terms[at(sign * j)]
+                copy(joined.at[slot], arrived.at[my_src], z_send, z_recv, {"src": at(sign * j)})
+        total = terms[my_src]
+        drain(arrived, z_recv, 2 * near + 1)
+        for j in near_js:
+            total = total + arrived[at(j)]
+        drain(arrived, z_send, 2 * near + 1)
+        drain(relayed, relay_send, 2 * near)
+        return total
+
     def scatter_start():
         for peer in src_peers:
             copy(terms.at[peer], arrived.at[my_src], z_send, z_recv, {"src": peer})
@@ -188,15 +218,17 @@
 
         forward_terms(coef)
         if outer == 0:
-            pl.semaphore_wait(barrier, n_src + n_plane - 2)
-        scatter_start()
-        if outer == 0:
+            pl.semaphore_wait(barrier, 2 * near + n_plane - 1)
             loads[3].wait()
-        misfit = scatter_finish() - obs[...]
+            misfit = first_scatter() - obs[...]
+        else:
+            scatter_start()
+            misfit = scatter_finish() - obs[...]
         gather_start(misfit, gathered_m)
         if outer + 1 == GN_STEPS:
             misfit_ref[...] = misfit
-        drain(terms, z_send, n_src)
+        if outer > 0:
+            drain(terms, z_send, n_src)
         drain(gathered_m, f_recv, n_src)
         adjoint_terms(gathered_m, adj_g)
         gauge_start(adj_g, 0)
@@ -246,6 +278,11 @@
         theta = theta + (alpha0[None] * d0 + alpha1[None] * (res + beta[None] * d0))
         drain(plane_b, p_send.at[1], n_plane)
     theta_ref[...] = theta
+
+
+def hand_over(theta_in, misfit_in, theta_out, misfit_out):
+    theta_out[...] = theta_in[...]
+    misfit_out[...] = misfit_in[...]
 
 
 def local(sizes, responses, footprint, theta_start, observed):
@@ -282,7 +319,9 @@
             pltpu.VMEM((n_src,) + row, F32),
             pltpu.VMEM((n_tile * n_gauge,) + row, F32),
             pltpu.VMEM((n_tile * n_gauge,) + row, F32),
-            dma((4,)), dma, dma, dma, dma,
+            pltpu.VMEM((n_src // 2, ens, length), F32),
+            pltpu.VMEM((n_src // 2, ens, length), F32),
+            dma((4,)), dma, dma((2,)), dma, dma, dma, dma,
             dma((2,)), dma((2,)), dma((2,)), dma((2,)), dma((2,)), dma((2,)),
         ],
         compiler_params=pltpu.CompilerParams(collective_id=0, has_side_effects=True),
@@ -292,6 +331,15 @@
         theta_start,
         observed.reshape(ens, length),
     )
+    theta, misfit = pl.pallas_call(
+        hand_over,
+        out_shape=(
+            jax.ShapeDtypeStruct(theta_start.shape, F32),
+            jax.ShapeDtypeStruct((ens, length), F32),
+        ),
+        in_specs=[vmem, vmem],
+        out_specs=(vmem, vmem),
+    )(theta, misfit)
     return theta, misfit.reshape(observed.shape)
 
 

time: 139 us -> 140 us (level)
  Pallas kernels: 137 us -> 140 us
  local copies, waits for them, and re-layouts: 1.93 us -> 0 us
    unnamed x4 -> x0, local copies, waits for them, and re-layouts: 1.93 us -> none
    pallas_call x1, Pallas kernels: 137 us -> 138 us  [local(): pl.pallas_call(functools.partial(kernel, (n_src, n_tile, n_gauge, src_dev...]
where the time goes in v3:
time: 140 us
  Pallas kernels  140 us (100%)
    pallas_call x1, Pallas kernels, local(): pl.pallas_call(functools.partial(kernel, (n_src, n_tile, n_gauge, src_dev...  138 us

profile of v3, /device:TPU:1, one launch (start us, length us, event | category | flops | bytes accessed | tf_op | source)
XLA Modules:
  0.0 140.3 jit_solution(11655923638380969864)
XLA Ops:
  0.6 138.4 %shard_map.59 = (f32[4,8,128]{2,1,0:T(8,128)}, f32[8,256]{1,0:T(8,128)}) custom-call(f32[8,128,256]{2,1,0:T(8,128)} %bitcast.4, s32[2,4]{1,0:T(2,128)} %bitcast.6, f32[4,8,128]{2,1,0:T(8,128)} %theta_hbm.1, f32[8,256]{1,0:T(8,128)} %bitcast.5), custom_call_target="tpu_custom_call" | custom-call | tf_op jit(solution)/shard_map/pallas_call | solution.py:296
  139.0 1.3 shard_map.60

commit v4 on v2

v4 whole, which is shorter than its diff:
```python
import functools

import jax
import jax.numpy as jnp
from jax import lax
from jax.experimental import pallas as pl
from jax.experimental.pallas import tpu as pltpu
from jax.sharding import PartitionSpec as P

GN_STEPS = 2
DAMPING = 0.1
MESH = pl.DeviceIdType.MESH
F32 = jnp.float32
BF16 = jnp.bfloat16


def split(x):
    hi = x.astype(BF16)
    return hi, (x - hi.astype(F32)).astype(BF16)


def far_first(n):
    return sorted(range(1, n), key=lambda j: (-min(j, n - j), j))


def kernel(
    sizes,
    resp_hbm, foot_hbm, theta_hbm, obs_hbm,
    theta_ref, misfit_ref,
    raw, w, foot_ref, theta0, obs, load_sem, *scratch,
):
    n_src, n_tile, n_gauge, src_dev, foot = sizes
    blocks = src_dev * foot
    ens, width = theta0.shape[1:]
    half, lane_half = ens // 2, obs.shape[1] // 2
    my_src, my_tile, my_gauge = lax.axis_index("src"), lax.axis_index("tile"), lax.axis_index("gauge")

    src_peers = [lax.rem(my_src + j, n_src) for j in far_first(n_src)]
    gauge_peers = [lax.rem(my_gauge + j, n_gauge) for j in far_first(n_gauge)]

    def hops(ab):
        a, b = ab[0] // 2, ab[1]
        return -(min(a, n_tile // 2 - a) + min(b, n_gauge - b))

    plane_peers = [
        {"tile": lax.rem(my_tile + a, n_tile), "gauge": lax.rem(my_gauge + b, n_gauge)}
        for a, b in sorted([(a, b) for a in range(n_tile) for b in range(n_gauge) if a or b], key=hops)
    ]
    my_plane = my_tile * n_gauge + my_gauge
    n_plane = n_tile * n_gauge

    loads = [
        pltpu.make_async_copy(a, b, load_sem.at[i])
        for i, (a, b) in enumerate(
            [(theta_hbm, theta0), (foot_hbm, foot_ref)]
            + [(resp_hbm.at[pl.ds(s * foot, foot)], raw.at[pl.ds(s * foot, foot)]) for s in range(src_dev)]
            + [(obs_hbm, obs)]
        )
    ]
    for load in loads:
        load.start()

    barrier = pltpu.get_barrier_semaphore()
    for peer in [{"src": p} for p in src_peers] + plane_peers:
        pl.semaphore_signal(barrier, inc=1, device_id=peer, device_id_type=MESH)

    lanes = lax.broadcasted_iota(jnp.int32, (ens, 128), 1)
    sub = lax.broadcasted_iota(jnp.int32, (ens, 128), 0)
    upper = sub < half
    place = jnp.where(upper, sub, sub - half)

    def swap(x):
        return pltpu.roll(x, half, 0)

    def to_row(values):
        out = jnp.zeros((ens, 128), F32)
        for i, v in enumerate(values):
            out = out + jnp.where(lanes == place + i * half, v, 0.0)
        return jnp.sum(out, axis=0, keepdims=True)

    def from_row(row, i):
        return jnp.sum(jnp.where(lanes == place + i * half, row, 0.0), axis=1, keepdims=True)

    def copy(src, dst, send_sem, recv_sem, peer):
        pltpu.make_async_remote_copy(
            src_ref=src, dst_ref=dst, send_sem=send_sem, recv_sem=recv_sem,
            device_id=peer, device_id_type=MESH,
        ).start()

    def drain(ref, sem, n):
        part = ref.at[pl.ds(0, n - 1)]
        pltpu.make_async_copy(part, part, sem).wait()

    def tree(parts):
        while len(parts) > 1:
            parts = [sum(parts[i:i + 2]) for i in range(0, len(parts), 2)]
        return parts[0]

    def sum_of(ref, n):
        return tree([ref[i] for i in range(n)])

    def inner(a, b):
        return 0.5 * jnp.sum(tree([a[s] * b[s] for s in range(src_dev)]), axis=1, keepdims=True)

    def inner_tile(a, b):
        return jnp.sum(a * b, axis=1, keepdims=True)

    def products(x):
        outs = []
        for s in range(src_dev):
            hi, lo = split(x[s])
            left = jnp.concatenate(
                [jnp.concatenate([hi, hi], axis=1), jnp.concatenate([lo, lo], axis=1)], axis=0
            )
            for f in range(foot):
                out = jnp.dot(left, w[s * foot + f], preferred_element_type=F32)
                out = out[0:ens] + out[ens:2 * ens]
                outs.append(jnp.where(upper, out[:, 0:lane_half], out[:, lane_half:]))
        return outs

    results = {}

    def chain(h, refs):
        (
            terms, arrived, field, gathered_m, gathered_b, adj_g, adj_p,
            rows_out, rows_in, scal_in, plane_a, plane_b,
            z_send, z_recv, f_send, f_recv, y_send, y_recv, r_send, r_recv, p_send, p_recv,
        ) = refs

        def scatter_start(outs):
            names = [jnp.full((ens, lane_half), foot_ref[b % foot, b // foot], jnp.int32) for b in range(blocks)]
            for slot, peer in enumerate(src_peers + [my_src]):
                total = tree([jnp.where(names[b] == peer, outs[b], 0.0) for b in range(blocks)])
                if slot < n_src - 1:
                    terms[slot] = total
                    copy(terms.at[slot], arrived.at[my_src], z_send, z_recv, {"src": peer})
                else:
                    arrived[my_src] = total

        def scatter_finish():
            drain(arrived, z_recv, n_src)
            return sum_of(arrived, n_src)

        def gather_start(value, dst):
            field[0] = value
            for peer in src_peers:
                copy(field.at[0], dst.at[my_src], f_send, f_recv, {"src": peer})
            dst[my_src] = value

        def adjoint_terms(src, dst):
            for s in range(src_dev):
                total = None
                for f in range(foot):
                    x = src[foot_ref[f, s]]
                    x = jnp.concatenate([jnp.where(upper, x, 0.0), jnp.where(upper, 0.0, x)], axis=1)
                    out = lax.dot_general(
                        jnp.concatenate(split(x), axis=0), w[s * foot + f],
                        (((1,), (1,)), ((), ())), preferred_element_type=F32,
                    )
                    out = out[0:ens] + out[ens:2 * ens]
                    out = out[:, 0:width] + out[:, width:2 * width]
                    total = out if total is None else total + out
                dst[my_gauge, s] = total

        def gauge_start(dst, i):
            for peer in gauge_peers:
                copy(dst.at[my_gauge], dst.at[my_gauge], y_send.at[i], y_recv.at[i], {"gauge": peer})

        def gauge_finish(dst, i):
            drain(dst, y_recv.at[i], n_gauge)
            total = sum_of(dst, n_gauge)
            return jnp.stack([total[s] + swap(total[s]) for s in range(src_dev)])

        def rows_start(row, dst, i):
            rows_out[i] = row
            for peer in src_peers:
                copy(rows_out.at[i], dst.at[my_src], r_send.at[i], r_recv.at[i], {"src": peer})
            dst[my_src] = row

        def rows_finish(dst, i):
            drain(dst, r_recv.at[i], n_src)
            return sum_of(dst, n_src)

        def plane_start(row, dst, i):
            rows_out[2 + i] = row
            for peer in plane_peers:
                copy(rows_out.at[2 + i], dst.at[my_plane], p_send.at[i], p_recv.at[i], peer)
            dst[my_plane] = row

        def plane_finish(dst, i):
            drain(dst, p_recv.at[i], n_plane)
            return sum_of(dst, n_plane)

        both = [theta0[s] for s in range(src_dev)]
        if h == 0:
            theta = jnp.stack([jnp.where(upper, t, swap(t)) for t in both])
        else:
            theta = jnp.stack([jnp.where(upper, swap(t), t) for t in both])

        for outer in range(GN_STEPS):
            slope = jax.nn.sigmoid(theta)
            coef = jnp.maximum(theta, 0.0) + jnp.log1p(jnp.exp(-jnp.abs(theta)))
            outs = products(coef)
            if outer == 0 and h == 0:
                pl.semaphore_wait(barrier, n_src + n_plane - 2)
            scatter_start(outs)
            yield

            if outer == 0 and h == 0:
                loads[2 + src_dev].wait()
            first, second = obs[:, 0:lane_half], obs[:, lane_half:]
            seen = jnp.where(upper, first, swap(second)) if h == 0 else jnp.where(upper, swap(first), second)
            misfit = scatter_finish() - seen
            gather_start(misfit, gathered_m)
            results["misfit", h] = misfit
            drain(terms, z_send, n_src)
            yield

            drain(gathered_m, f_recv, n_src)
            adjoint_terms(gathered_m, adj_g)
            gauge_start(adj_g, 0)
            drain(gathered_m, f_send, n_src)
            yield

            d0 = -(slope * gauge_finish(adj_g, 0) + DAMPING * theta)
            scatter_start(products(slope * d0))
            rows_start(to_row([inner(d0, d0)]), rows_in, 0)
            drain(adj_g, y_send.at[0], n_gauge)
            yield

            b0 = scatter_finish()
            gather_start(b0, gathered_b)
            drain(terms, z_send, n_src)
            yield

            drain(gathered_b, f_recv, n_src)
            adjoint_terms(gathered_b, adj_p)
            gauge_start(adj_p, 1)
            rr_row = rows_finish(rows_in, 0)
            drain(rows_in, r_send.at[0], n_src)
            squares = tree([gathered_b[t] * gathered_b[t] for t in range(n_src)])
            bb_row = to_row([jnp.sum(squares, axis=1, keepdims=True)])
            plane_start(bb_row + jnp.where(lanes[0:1] < half, 0.0, pltpu.roll(rr_row, half, 1)), plane_a, 0)
            drain(gathered_b, f_send, n_src)
            yield

            p = slope * gauge_finish(adj_p, 1) + DAMPING * d0
            scatter_start(products(slope * p))
            drain(adj_p, y_send.at[1], n_gauge)
            yield

            row = plane_finish(plane_a, 0)
            bb, rr0 = from_row(row, 0), from_row(row, 1) * (1.0 / n_gauge)
            alpha0 = rr0 / (bb + DAMPING * rr0)
            res = d0 - alpha0[None] * p
            rr1, rd = inner(res, res), inner(res, d0)
            drain(plane_a, p_send.at[0], n_plane)
            image = b0 - alpha0 * scatter_finish()
            rows_start(to_row([inner_tile(image, image), inner_tile(image, b0), rr1, rd]), scal_in, 1)
            drain(terms, z_send, n_src)
            yield

            plane_start(rows_finish(scal_in, 1), plane_b, 1)
            drain(scal_in, r_send.at[1], n_src)
            yield

            row = plane_finish(plane_b, 1)
            cc, cb = from_row(row, 0), from_row(row, 1)
            rr1, rd = from_row(row, 2) * (1.0 / n_gauge), from_row(row, 3) * (1.0 / n_gauge)
            beta = rr1 / rr0
            curv = cc + beta * (2.0 * cb + beta * bb) + DAMPING * (rr1 + beta * (2.0 * rd + beta * rr0))
            alpha1 = rr1 / curv
            theta = theta + (alpha0[None] * d0 + alpha1[None] * (res + beta[None] * d0))
            drain(plane_b, p_send.at[1], n_plane)
        results["theta", h] = theta

    loads[0].wait()
    loads[1].wait()
    for b in range(blocks):
        if b % foot == 0:
            loads[2 + b // foot].wait()
        hi, lo = split(raw[b])
        w[b, 0:width, :] = hi
        w[b, width:2 * width, :] = lo

    each = len(scratch) // 2
    running = [chain(h, scratch[h * each:(h + 1) * each]) for h in range(2)]
    while running:
        running = [c for c in running if next(c, True) is None]

    for s in range(src_dev):
        theta_ref[s] = jnp.where(upper, results["theta", 0][s], results["theta", 1][s])
    one, two = results["misfit", 0], results["misfit", 1]
    misfit_ref[:, 0:lane_half] = jnp.where(upper, one, swap(two))
    misfit_ref[:, lane_half:] = jnp.where(upper, swap(one), two)


def hand_over(theta_in, misfit_in, theta_out, misfit_out):
    theta_out[...] = theta_in[...]
    misfit_out[...] = misfit_in[...]


def local(sizes, responses, footprint, theta_start, observed):
    n_src, n_tile, n_gauge = sizes
    src_dev, foot, _, width, length = responses.shape
    ens = theta_start.shape[1]
    blocks = src_dev * foot
    vmem, anywhere = pl.BlockSpec(memory_space=pltpu.VMEM), pl.BlockSpec(memory_space=pl.ANY)
    dma = pltpu.SemaphoreType.DMA
    row, packed = (1, 128), (ens, length // 2)
    theta, misfit = pl.pallas_call(
        functools.partial(kernel, (n_src, n_tile, n_gauge, src_dev, foot)),
        out_shape=(
            jax.ShapeDtypeStruct(theta_start.shape, F32),
            jax.ShapeDtypeStruct((ens, length), F32),
        ),
        in_specs=[anywhere] * 4,
        out_specs=(vmem, vmem),
        scratch_shapes=[
            pltpu.VMEM((blocks, width, length), F32),
            pltpu.VMEM((blocks, 2 * width, length), BF16),
            pltpu.SMEM((foot, src_dev), jnp.int32),
            pltpu.VMEM((src_dev, ens, width), F32),
            pltpu.VMEM((ens, length), F32),
            dma((3 + src_dev,)),
        ] + 2 * [
            pltpu.VMEM((n_src - 1,) + packed, F32),
            pltpu.VMEM((n_src,) + packed, F32),
            pltpu.VMEM((1,) + packed, F32),
            pltpu.VMEM((n_src,) + packed, F32),
            pltpu.VMEM((n_src,) + packed, F32),
            pltpu.VMEM((n_gauge, src_dev, ens, width), F32),
            pltpu.VMEM((n_gauge, src_dev, ens, width), F32),
            pltpu.VMEM((4,) + row, F32),
            pltpu.VMEM((n_src,) + row, F32),
            pltpu.VMEM((n_src,) + row, F32),
            pltpu.VMEM((n_tile * n_gauge,) + row, F32),
            pltpu.VMEM((n_tile * n_gauge,) + row, F32),
            dma, dma, dma, dma,
            dma((2,)), dma((2,)), dma((2,)), dma((2,)), dma((2,)), dma((2,)),
        ],
        compiler_params=pltpu.CompilerParams(collective_id=0, has_side_effects=True),
    )(
        responses.reshape(blocks, width, length),
        footprint.T,
        theta_start,
        observed.reshape(ens, length),
    )
    theta, misfit = pl.pallas_call(
        hand_over,
        out_shape=(
            jax.ShapeDtypeStruct(theta_start.shape, F32),
            jax.ShapeDtypeStruct((ens, length), F32),
        ),
        in_specs=[vmem, vmem],
        out_specs=(vmem, vmem),
    )(theta, misfit)
    return theta, misfit.reshape(observed.shape)


def solution(mesh):
    sizes = (mesh.shape["src"], mesh.shape["tile"], mesh.shape["gauge"])
    in_specs = (
        P(("src", "tile"), None, "gauge", None, None),
        P(("src", "tile"), None),
        P(("src", "tile"), None, None),
        P(("src", "tile"), "gauge", None, None),
    )
    out_specs = (P(("src", "tile"), None, None), P(("src", "tile"), "gauge", None, None))
    return jax.shard_map(
        functools.partial(local, sizes), mesh=mesh, in_specs=in_specs, out_specs=out_specs, check_vma=False
    )
```

time: 139 us -> 135 us (0.971)
  Pallas kernels: 137 us -> 134 us
  local copies, waits for them, and re-layouts: 1.93 us -> 0 us
    pallas_call x1, Pallas kernels: 137 us -> 133 us  [local(): pl.pallas_call(functools.partial(kernel, (n_src, n_tile, n_gauge, src_dev...]
    unnamed x4 -> x0, local copies, waits for them, and re-layouts: 1.93 us -> none
where the time goes in v4:
time: 135 us
  Pallas kernels  134 us (99%)
    pallas_call x1, Pallas kernels, local(): pl.pallas_call(functools.partial(kernel, (n_src, n_tile, n_gauge, src_dev...  133 us

profile of v4, /device:TPU:1, one launch (start us, length us, event | category | flops | bytes accessed | tf_op | source)
XLA Modules:
  0.0 134.8 jit_solution(12370775982749152742)
XLA Ops:
  0.6 132.8 %shard_map.59 = (f32[4,8,128]{2,1,0:T(8,128)}, f32[8,256]{1,0:T(8,128)}) custom-call(f32[8,128,256]{2,1,0:T(8,128)} %bitcast.4, s32[2,4]{1,0:T(2,128)} %bitcast.6, f32[4,8,128]{2,1,0:T(8,128)} %theta_hbm.1, f32[8,256]{1,0:T(8,128)} %bitcast.5), custom_call_target="tpu_custom_call" | custom-call | tf_op jit(solution)/shard_map/pallas_call | solution.py:311
  133.5 1.3 shard_map.60

commit v5 on v4

--- a/solution.py
+++ b/solution.py
@@ -148,6 +148,7 @@
             dst[my_src] = value
 
         def adjoint_terms(src, dst):
+            sums = []
             for s in range(src_dev):
                 total = None
                 for f in range(foot):
@@ -160,7 +161,9 @@
                     out = out[0:ens] + out[ens:2 * ens]
                     out = out[:, 0:width] + out[:, width:2 * width]
                     total = out if total is None else total + out
-                dst[my_gauge, s] = total
+                sums.append(total + swap(total))
+            for pair in range(src_dev // 2):
+                dst[my_gauge, pair] = jnp.where(upper, sums[2 * pair], sums[2 * pair + 1])
 
         def gauge_start(dst, i):
             for peer in gauge_peers:
@@ -169,7 +172,11 @@
         def gauge_finish(dst, i):
             drain(dst, y_recv.at[i], n_gauge)
             total = sum_of(dst, n_gauge)
-            return jnp.stack([total[s] + swap(total[s]) for s in range(src_dev)])
+            out = []
+            for pair in range(src_dev // 2):
+                turned = swap(total[pair])
+                out += [jnp.where(upper, total[pair], turned), jnp.where(upper, turned, total[pair])]
+            return jnp.stack(out)
 
         def rows_start(row, dst, i):
             rows_out[i] = row
@@ -224,6 +231,8 @@
 
             d0 = -(slope * gauge_finish(adj_g, 0) + DAMPING * theta)
             scatter_start(products(slope * d0))
+            yield
+
             rows_start(to_row([inner(d0, d0)]), rows_in, 0)
             drain(adj_g, y_send.at[0], n_gauge)
             yield
@@ -236,6 +245,8 @@
             drain(gathered_b, f_recv, n_src)
             adjoint_terms(gathered_b, adj_p)
             gauge_start(adj_p, 1)
+            yield
+
             rr_row = rows_finish(rows_in, 0)
             drain(rows_in, r_send.at[0], n_src)
             squares = tree([gathered_b[t] * gathered_b[t] for t in range(n_src)])
@@ -329,8 +340,8 @@
             pltpu.VMEM((1,) + packed, F32),
             pltpu.VMEM((n_src,) + packed, F32),
             pltpu.VMEM((n_src,) + packed, F32),
-            pltpu.VMEM((n_gauge, src_dev, ens, width), F32),
-            pltpu.VMEM((n_gauge, src_dev, ens, width), F32),
+            pltpu.VMEM((n_gauge, src_dev // 2, ens, width), F32),
+            pltpu.VMEM((n_gauge, src_dev // 2, ens, width), F32),
             pltpu.VMEM((4,) + row, F32),
             pltpu.VMEM((n_src,) + row, F32),
             pltpu.VMEM((n_src,) + row, F32),

time: 135 us -> 134 us (level)
  no operation moved by 1% of the time
where the time goes in v5:
time: 134 us
  Pallas kernels  133 us (99%)
    pallas_call x1, Pallas kernels, local(): pl.pallas_call(functools.partial(kernel, (n_src, n_tile, n_gauge, src_dev...  132 us

profile of v5, /device:TPU:1, one launch (start us, length us, event | category | flops | bytes accessed | tf_op | source)
XLA Modules:
  0.0 133.9 jit_solution(12913521525550091224)
XLA Ops:
  0.6 131.9 %shard_map.59 = (f32[4,8,128]{2,1,0:T(8,128)}, f32[8,256]{1,0:T(8,128)}) custom-call(f32[8,128,256]{2,1,0:T(8,128)} %bitcast.4, s32[2,4]{1,0:T(2,128)} %bitcast.6, f32[4,8,128]{2,1,0:T(8,128)} %theta_hbm.1, f32[8,256]{1,0:T(8,128)} %bitcast.5), custom_call_target="tpu_custom_call" | custom-call | tf_op jit(solution)/shard_map/pallas_call | solution.py:322
  132.5 1.3 shard_map.60
